TPU v7x, 32 devices: a whole 2x2x4 slice. The times are simulated.
32 devices in a mesh: mp: 2 (over y), survey: 16 (over z, x, core).
Axes of the slice: x: 2, y: 2, z: 4, core: 2. Of those that a mesh axis runs over, the one named last changes fastest.
Arguments:
- model: bfloat16 [64, 64, 128], P(('mp', 'survey')), may hold values from -6 to 6
- observed: bfloat16 [32, 64, 128], P(('mp', 'survey')), may hold values from -6 to 6
- weights: bfloat16 [32, 64, 128], P(('mp', 'survey')), may hold values from 0.29882812 to 3
- sensitivity: bfloat16 [2, 2048, 128, 128], P('mp', 'survey'), may hold values from -0.046875 to 0.046875
- block_rows: int32 [2, 2048], P('mp', 'survey'), may hold values from 0 to 15
- block_cols: int32 [2, 2048], P('mp', 'survey'), may hold values from 0 to 3
- block_count: int32 [2, 16], P('mp', 'survey'), may hold values from 32 to 128, as said below
Outputs:
- gradient: float32 [64, 64, 128], P(('mp', 'survey'))
Inputs may be any that keep to these rules, and one draw needn't show every extreme that they name: `block_count`: some device uses all 128 slots.
All inputs are finite; a program needn't handle non-finite values.
Results may differ from a plain program's by a relative error of at most 0.0017.
Values may be sent and summed in bfloat16 or wider, within the bound.
A program may use at most 64 MiB of HBM per device.

v0:
```python
import jax
import jax.numpy as jnp
from jax import lax
from jax.sharding import PartitionSpec as P

SMOOTH = 0.5


def smoothing(model):
    field_f32 = model.astype(jnp.float32)
    earlier = jnp.concatenate([field_f32[:, :1], field_f32[:, :-1]], axis=1)
    later_step = jnp.concatenate([field_f32[:, 1:], field_f32[:, -1:]], axis=1)
    return SMOOTH * (2.0 * field_f32 - earlier - later_step)


def collect(target_ids, in_use, terms, count):
    spare_ids = jnp.where(in_use, target_ids, count)
    summed = jax.ops.segment_sum(terms, spare_ids, num_segments=count + 1)
    return summed[:count]


def on_device(model, observed, weights, sensitivity, block_rows, block_cols, block_count):
    blocks = sensitivity[0]
    row_ids = block_rows[0]
    col_ids = block_cols[0]
    slots = blocks.shape[0]
    in_use = jnp.arange(slots, dtype=jnp.int32) < block_count[0, 0]
    group_rows = observed.shape[0] * lax.axis_size("survey")
    slab = lax.all_gather(model, "mp", axis=0, tiled=True)
    slab_rows = slab.shape[0]
    picked = jnp.take(slab, col_ids, axis=0)
    terms = jnp.einsum("ktc,krc->ktr", picked, blocks, preferred_element_type=jnp.float32)
    partial_value = collect(row_ids, in_use, terms, group_rows)
    summed = lax.psum(partial_value, "survey")
    seen_data, data_weight = (
        lax.all_gather(observed, "survey", axis=0, tiled=True),
        lax.all_gather(weights, "survey", axis=0, tiled=True),
    )
    residual = (data_weight.astype(jnp.float32) * (summed - seen_data.astype(jnp.float32))).astype(
        jnp.bfloat16
    )
    resid_rows = jnp.take(residual, row_ids, axis=0)
    back_terms = jnp.einsum("ktr,krc->ktc", resid_rows, blocks, preferred_element_type=jnp.float32)
    gradient_slab = collect(col_ids, in_use, back_terms, slab_rows)
    owned = lax.psum_scatter(gradient_slab, "mp", scatter_dimension=0, tiled=True)
    return owned + smoothing(model)


def solution(mesh):
    in_specs = (
        P(("mp", "survey"), None, None),
        P(("mp", "survey"), None, None),
        P(("mp", "survey"), None, None),
        P("mp", "survey", None, None),
        P("mp", "survey"),
        P("mp", "survey"),
        P("mp", "survey"),
    )
    out_specs = P(("mp", "survey"), None, None)
    return jax.shard_map(
        on_device, mesh=mesh, in_specs=in_specs, out_specs=out_specs, check_vma=False
    )
```

profile of v0, /device:TPU:0, one launch (start us, length us, event | category | flops | bytes accessed | tf_op | source)
XLA Modules:
  0.0 170.1 jit_solution(15884253694293784097)
XLA Ops:
  6.5 0.0 all-reduce.2.cloned.1.call-start
  7.2 0.7 compare_and_fusion
  7.9 0.7 fusion.15
  8.5 5.8 %all_gather.10 = bf16[4,64,128]{2,1,0:T(8,128)(2,1)S(1)} all-gather(bf16[2,64,128]{2,1,0:T(8,128)(2,1)} %param.7), channel_id=1, replica_groups=mesh['mp'=2,'survey'=16] {'mp'}, dimensions={0}, use_global_device_ids=true | all-gather | bytes 98304 | tf_op jit(solution)/shard_map/all_gather | solution.py:29
  14.3 0.0 copy-start.3
  14.3 0.9 gather_fusion
  15.3 0.0 copy-done.3
  15.3 7.1 %fusion.2 = f32[128,64,128]{2,1,0:T(8,128)} fusion(bf16[1,128,128,128]{3,2,1,0:T(8,128)(2,1)} %param.10, bf16[128,64,128]{2,1,0:T(8,128)(2,1)S(1)} %gather_fusion, pred[128]{0:T(512)(128)(4,1)S(1)} %compare_and_fusion), kind=kOutput, calls=%fused_computation.6 | convolution fusion | flops 269484032 | bytes 10485888 | tf_op jit(solution)/shard_map/ktc,krc->ktr/dot_general | solution.py:32
  22.4 0.0 copy-start.1
  22.4 0.0 copy-start.2
  22.4 13.6 %scatter_fusion = f32[17,64,128]{2,1,0:T(8,128)S(1)} fusion(f32[17,64,128]{2,1,0:T(8,128)S(1)} %broadcast_in_dim.36, s32[128]{0:T(128)S(1)} %get-tuple-element.10, f32[128,64,128]{2,1,0:T(8,128)} %fusion.2), kind=kCustom, calls=%fused_computation.2 | custom fusion | flops 1048576 | bytes 12583424 | tf_op jit(solution)/shard_map/scatter-add | solution.py:18
  36.0 0.8 slice.28
  36.8 0.0 all-reduce.2.cloned.1.call-update
  36.8 0.0 reduce-scatter.2.cloned.1.call-start
  36.9 0.0 copy-done.1
  36.9 23.0 %all_gather.11 = bf16[16,64,128]{2,1,0:T(8,128)(2,1)S(1)} all-gather(bf16[1,64,128]{2,1,0:T(8,128)(2,1)S(1)} %copy-done.1), channel_id=1, replica_groups=mesh['mp'=2,'survey'=16] {'survey'}, dimensions={0}, use_global_device_ids=true | all-gather | bytes 278528 | tf_op jit(solution)/shard_map/all_gather | solution.py:36
  59.9 0.0 copy-done.2
  59.9 18.2 %all_gather.9 = bf16[16,64,128]{2,1,0:T(8,128)(2,1)S(1)} all-gather(bf16[1,64,128]{2,1,0:T(8,128)(2,1)S(1)} %copy-done.2), channel_id=1, replica_groups=mesh['mp'=2,'survey'=16] {'survey'}, dimensions={0}, use_global_device_ids=true | all-gather | bytes 278528 | tf_op jit(solution)/shard_map/all_gather | solution.py:37
  78.1 51.0 %all-reduce.2.cloned.1.call-done = f32[16,64,128]{2,1,0:T(8,128)} async-done(((f32[16,64,128]{2,1,0:T(8,128)}), f32[16,64,128]{2,1,0:T(8,128)}) %all-reduce.2.cloned.1.call-update) | async-done | bytes 524304 | tf_op jit(solution)/shard_map/psum | solution.py:34
  129.1 1.1 multiply_convert_fusion
  130.2 1.0 gather_fusion.1
  131.2 5.4 %fusion = f32[128,64,128]{2,1,0:T(8,128)} fusion(bf16[1,128,128,128]{3,2,1,0:T(8,128)(2,1)} %param.10, bf16[128,64,128]{2,1,0:T(8,128)(2,1)S(1)} %gather_fusion.1, pred[128]{0:T(512)(128)(4,1)S(1)} %compare_and_fusion.1), kind=kOutput, calls=%fused_computation.4 | convolution fusion | flops 269484032 | bytes 10485888 | tf_op jit(solution)/shard_map/ktr,krc->ktc/dot_general | solution.py:43
  136.6 0.0 copy-start
  136.6 13.6 %scatter_fusion.1 = f32[5,64,128]{2,1,0:T(8,128)S(1)} fusion(f32[5,64,128]{2,1,0:T(8,128)S(1)} %broadcast_in_dim.33, s32[128]{0:T(128)S(1)} %get-tuple-element.12, f32[128,64,128]{2,1,0:T(8,128)} %fusion), kind=kCustom, calls=%fused_computation.3 | custom fusion | flops 1048576 | bytes 12583424 | tf_op jit(solution)/shard_map/scatter-add | solution.py:18
  150.2 0.7 slice.29
  150.9 0.0 reduce-scatter.2.cloned.1.call-update
  150.9 0.0 copy-done
  150.9 10.9 %reduce-scatter.2.cloned.1.call-done = f32[2,64,128]{2,1,0:T(8,128)} async-done(((f32[4,64,128]{2,1,0:T(8,128)}), f32[2,64,128]{2,1,0:T(8,128)}) %reduce-scatter.2.cloned.1.call-update) | async-done | bytes 65552 | tf_op jit(solution)/shard_map/reduce_scatter | solution.py:45
  161.8 1.5 fusion.12
  (8 shorter events, 0.1 us)
Async XLA Ops:
  6.5 122.6 %all-reduce.2.cloned.1.call-start = ((), (), s32[]{:S(2)}) async-start(), calls=%async_computation.1 | async-start | bytes 1048576 | tf_op jit(solution)/shard_map/psum | solution.py:34
  14.3 1.0 copy-start.3
  22.4 14.5 %copy-start.1 = (bf16[1,64,128]{2,1,0:T(8,128)(2,1)S(1)}, bf16[1,64,128]{2,1,0:T(8,128)(2,1)}, u32[]{:S(2)}) copy-start(bf16[1,64,128]{2,1,0:T(8,128)(2,1)} %param.8) | copy-start | bytes 49156
  22.4 37.5 %copy-start.2 = (bf16[1,64,128]{2,1,0:T(8,128)(2,1)S(1)}, bf16[1,64,128]{2,1,0:T(8,128)(2,1)}, u32[]{:S(2)}) copy-start(bf16[1,64,128]{2,1,0:T(8,128)(2,1)} %param.9) | copy-start | bytes 49156
  36.8 125.0 %reduce-scatter.2.cloned.1.call-start = ((), (), s32[]{:S(2)}) async-start(), calls=%async_computation.2 | async-start | bytes 196608 | tf_op jit(solution)/shard_map/reduce_scatter | solution.py:45
  136.6 14.3 %copy-start = (bf16[2,64,128]{2,1,0:T(8,128)(2,1)S(1)}, bf16[2,64,128]{2,1,0:T(8,128)(2,1)}, u32[]{:S(2)}) copy-start(bf16[2,64,128]{2,1,0:T(8,128)(2,1)} %param.7) | copy-start | bytes 98308
Sparse Core Ops, SparseCore 0:
  37.0 92.0 all-reduce.1
  151.0 10.7 reduce-scatter.1
where the time goes:
time: 171 us; the launch traced here: 170 us
  waiting for transfers between devices  61.9 us (36%)
  blocking collectives  46.9 us (27%)
  other arithmetic  31.1 us (18%)
  between operations  14.2 us (8%)
  matrix products  12.5 us (7%)
  local copies, waits for them, and re-layouts  3.49 us (2%)
    psum x1, waiting for transfers between devices, on_device(): summed = lax.psum(partial_value, 'survey')  51 us
    scatter-add x2, other arithmetic, collect(): summed = jax.ops.segment_sum(terms, spare_ids, num_segments=count + 1)  27.1 us
    all_gather x1, blocking collectives, on_device(): lax.all_gather(observed, 'survey', axis=0, tiled=True)  23 us
    all_gather x1, blocking collectives, on_device(): lax.all_gather(weights, 'survey', axis=0, tiled=True)  18.2 us
    reduce_scatter x1, waiting for transfers between devices, on_device(): lax.psum_scatter(gradient_slab, 'mp', scatter_dimension=0, tiled=True)  10.9 us
    dot_general x1, matrix products, on_device(): jnp.einsum('ktc,krc->ktr', picked, blocks, preferred_element_type=jnp.flo...  7.05 us
    all_gather x1, blocking collectives, on_device(): slab = lax.all_gather(model, 'mp', axis=0, tiled=True)  5.79 us
    dot_general x1, matrix products, on_device(): jnp.einsum('ktr,krc->ktc', resid_rows, blocks, preferred_element_type=jnp...  5.4 us
  transfers between devices with their start and end apart: 2, of which 2 were waited for; matrix products, arithmetic and copies ran while one was open for 0% of the time, Pallas kernels for 0%

commit v1 on v0

v1 whole, which is shorter than its diff:
```python
import functools

import jax
import jax.numpy as jnp
from jax import lax
from jax.experimental import pallas as pl
from jax.experimental.pallas import tpu as pltpu
from jax.sharding import PartitionSpec as P

SMOOTH = 0.5
MESH = pl.DeviceIdType.MESH
PARTS = 8
UNROLL = 8


def smoothing(field):
    steps = field.shape[0]
    at = lax.broadcasted_iota(jnp.int32, field.shape, 0)
    earlier = jnp.where(at == 0, field, pltpu.roll(field, 1, 0))
    later_step = jnp.where(at == steps - 1, field, pltpu.roll(field, steps - 1, 0))
    return SMOOTH * (2.0 * field - earlier - later_step)


def kernel(
    n_mp,
    n_survey,
    rows_ref,
    cols_ref,
    row_links,
    col_links,
    model_ref,
    seen_ref,
    weight_ref,
    sens_hbm,
    out_ref,
    blocks,
    slab,
    chain,
    sib_send,
    sib_recv,
    chip_send,
    chip_recv,
    resid,
    grad_send,
    grad_recv,
    load_sem,
    model_sem,
    sib_sem,
    chip_sem,
    own_sem,
    gather_sem,
    relay_sem,
    grad_sem,
):
    m = lax.axis_index("mp")
    s = lax.axis_index("survey")
    chips = n_survey // 2
    chip, core = s // 2, s % 2
    sibling = (m, chip * 2 + 1 - core)
    slots = blocks.shape[0]
    owned = model_ref.shape[0]
    per = seen_ref.shape[0]

    def chip_at(j):
        return (chip + j) % chips

    def copy(src, dst, sems, j, device):
        return pltpu.make_async_remote_copy(
            src_ref=src,
            dst_ref=dst,
            send_sem=sems.at[0, j],
            recv_sem=sems.at[1, j],
            device_id=device,
            device_id_type=MESH,
        )

    step = slots // PARTS
    loads = [
        pltpu.make_async_copy(
            sens_hbm.at[pl.ds(i * step, step)], blocks.at[pl.ds(i * step, step)], load_sem.at[i]
        )
        for i in range(PARTS)
    ]
    for load in loads:
        load.start()

    barrier = pltpu.get_barrier_semaphore()
    partners = [((m + j) % n_mp, s) for j in range(1, n_mp)] + [sibling]
    partners += [(m, chip_at(j) * 2 + core) for j in range(1, chips)]
    for partner in partners:
        pl.semaphore_signal(barrier, inc=1, device_id=partner, device_id_type=MESH)
    pl.semaphore_wait(barrier, len(partners))

    here = pl.ds(m * owned, owned)
    sends = [
        copy(model_ref, slab.at[here], model_sem, j - 1, ((m + j) % n_mp, s))
        for j in range(1, n_mp)
    ]
    for send in sends:
        send.start()
    slab[here] = model_ref[...]
    for i in range(owned):
        out_ref[i] = smoothing(model_ref[i].astype(jnp.float32))
    chain[0] = jnp.zeros(chain.shape[1:], jnp.float32)
    for load in loads:
        load.wait()
    for send in sends:
        send.wait()

    def forward(g, carry):
        base = g * UNROLL
        terms = [
            lax.dot_general(
                slab[cols_ref[base + u]],
                blocks[base + u],
                (((1,), (1,)), ((), ())),
                preferred_element_type=jnp.float32,
            )
            for u in range(UNROLL)
        ]
        for u in range(UNROLL):
            chain[base + u + 1] = terms[u] + chain[row_links[base + u]]
        return carry

    lax.fori_loop(0, slots // UNROLL, forward, 0)

    order = list(range(1, chips)) + [0]
    swaps = {}
    for j in order:
        for i in range(per):
            sib_send[j, i] = chain[row_links[slots + (chip_at(j) * 2 + 1 - core) * per + i]]
        swaps[j] = copy(sib_send.at[j], sib_recv.at[j], sib_sem, j, sibling)
        swaps[j].start()
    scatters = {}
    for j in order:
        swaps[j].wait_recv()
        for i in range(per):
            mine = chain[row_links[slots + (chip_at(j) * 2 + core) * per + i]]
            chip_send[j, i] = mine + sib_recv[j, i]
        if j:
            scatters[j] = copy(
                chip_send.at[j], chip_recv.at[j], chip_sem, j, (m, chip_at(j) * 2 + core)
            )
            scatters[j].start()
    total = chip_send[0]
    for j in range(1, chips):
        scatters[j].wait_recv()
        total += chip_recv[j]

    value = weight_ref[...].astype(jnp.float32) * (total - seen_ref[...].astype(jnp.float32))
    mine = resid.at[pl.ds(s * per, per)]
    resid[pl.ds(s * per, per)] = value.astype(jnp.bfloat16)
    gathers = {}
    for j in range(1, chips):
        gathers[j] = copy(mine, mine, gather_sem, j, (m, chip_at(j) * 2 + core))
        gathers[j].start()
    own = copy(mine, mine, own_sem, 0, sibling)
    own.start()
    relays = {}
    for j in range(1, chips):
        gathers[j].wait_recv()
        source = resid.at[pl.ds((chip_at(chips - j) * 2 + core) * per, per)]
        relays[j] = copy(source, source, relay_sem, j, sibling)
        relays[j].start()
    own.wait_recv()
    for j in range(1, chips):
        relays[j].wait_recv()

    def backward(g, carry):
        base = g * UNROLL
        terms = [
            jnp.dot(
                resid[rows_ref[base + u]], blocks[base + u], preferred_element_type=jnp.float32
            )
            for u in range(UNROLL)
        ]
        for u in range(UNROLL):
            chain[base + u + 1] = terms[u] + chain[col_links[base + u]]
        return carry

    lax.fori_loop(0, slots // UNROLL, backward, 0)

    returns = {}
    for j in range(1, n_mp):
        owner = (m + j) % n_mp
        for i in range(owned):
            grad_send[j, i] = chain[col_links[slots + owner * owned + i]]
        returns[j] = copy(grad_send.at[j], grad_recv.at[j], grad_sem, j, (owner, s))
        returns[j].start()
    for i in range(owned):
        out_ref[i] += chain[col_links[slots + m * owned + i]]
    for j in range(1, n_mp):
        returns[j].wait_recv()
        out_ref[...] += grad_recv[j]

    own.wait_send()
    for group in (swaps, scatters, gathers, relays, returns):
        for sent in group.values():
            sent.wait_send()


def links(ids, in_use, count):
    slots = ids.shape[0]
    at = jnp.arange(slots, dtype=jnp.int32)
    wanted = jnp.concatenate([ids, jnp.arange(count, dtype=jnp.int32)])
    limit = jnp.concatenate([at, jnp.full((count,), slots, jnp.int32)])
    hit = (wanted[:, None] == ids[None, :]) & (at[None, :] < limit[:, None]) & in_use[None, :]
    return jnp.max(jnp.where(hit, at[None, :] + 1, 0), axis=1)


def on_device(
    n_mp, n_survey, model, observed, weights, sensitivity, block_rows, block_cols, block_count
):
    row_ids, col_ids = block_rows[0], block_cols[0]
    slots = row_ids.shape[0]
    owned, steps, cells = model.shape
    per = observed.shape[0]
    chips = n_survey // 2
    in_use = jnp.arange(slots, dtype=jnp.int32) < block_count[0, 0]
    row_links = links(row_ids, in_use, per * n_survey)
    col_links = links(col_ids, in_use, owned * n_mp)
    smem = pl.BlockSpec(memory_space=pltpu.SMEM)
    vmem = pl.BlockSpec(memory_space=pltpu.VMEM)
    pair = lambda n: pltpu.SemaphoreType.DMA((2, n))
    f32, bf16 = jnp.float32, jnp.bfloat16
    return pl.pallas_call(
        functools.partial(kernel, n_mp, n_survey),
        out_shape=jax.ShapeDtypeStruct(model.shape, f32),
        in_specs=[smem] * 4 + [vmem] * 3 + [pl.BlockSpec(memory_space=pl.ANY)],
        out_specs=vmem,
        scratch_shapes=[
            pltpu.VMEM(sensitivity.shape[1:], bf16),
            pltpu.VMEM((owned * n_mp, steps, cells), bf16),
            pltpu.VMEM((slots + 1, steps, cells), f32),
            pltpu.VMEM((chips, per, steps, cells), f32),
            pltpu.VMEM((chips, per, steps, cells), f32),
            pltpu.VMEM((chips, per, steps, cells), f32),
            pltpu.VMEM((chips, per, steps, cells), f32),
            pltpu.VMEM((per * n_survey, steps, cells), bf16),
            pltpu.VMEM((n_mp, owned, steps, cells), f32),
            pltpu.VMEM((n_mp, owned, steps, cells), f32),
            pltpu.SemaphoreType.DMA((PARTS,)),
            pair(n_mp),
            pair(chips),
            pair(chips),
            pair(1),
            pair(chips),
            pair(chips),
            pair(n_mp),
        ],
        compiler_params=pltpu.CompilerParams(
            collective_id=0, has_side_effects=True, vmem_limit_bytes=40 << 20
        ),
    )(row_ids, col_ids, row_links, col_links, model, observed, weights, sensitivity[0])


def solution(mesh):
    n_mp, n_survey = mesh.shape["mp"], mesh.shape["survey"]
    in_specs = (
        P(("mp", "survey"), None, None),
        P(("mp", "survey"), None, None),
        P(("mp", "survey"), None, None),
        P("mp", "survey", None, None),
        P("mp", "survey"),
        P("mp", "survey"),
        P("mp", "survey"),
    )
    out_specs = P(("mp", "survey"), None, None)
    return jax.shard_map(
        functools.partial(on_device, n_mp, n_survey),
        mesh=mesh,
        in_specs=in_specs,
        out_specs=out_specs,
        check_vma=False,
    )
```

time: 171 us -> 45.7 us (0.27)
  waiting for transfers between devices: 61.9 us -> 0 us
  blocking collectives: 46.9 us -> 0 us
  Pallas kernels: 0 us -> 35.2 us
  other arithmetic: 31.1 us -> 3.07 us
  between operations: 14.2 us -> 0.71 us
  matrix products: 12.5 us -> 0 us
  local copies, waits for them, and re-layouts: 3.49 us -> 6.32 us
    psum x1 -> x0, waiting for transfers between devices: 51 us -> none  [on_device(): summed = lax.psum(partial_value, 'survey')]
    all_gather x3 -> x0, blocking collectives: 46.9 us -> none  [the longest x1 23 us: on_device(): lax.all_gather(observed, 'survey', axis=0, tiled=True)]
    pallas_call x0 -> x1, Pallas kernels: none -> 35.2 us  [on_device(): pl.pallas_call(functools.partial(kernel, n_mp, n_survey), out_shape=jax.S...]
    scatter-add x2 -> x0, other arithmetic: 27.1 us -> none  [collect(): summed = jax.ops.segment_sum(terms, spare_ids, num_segments=count + 1)]
    dot_general x2 -> x0, matrix products: 12.5 us -> none  [the longest x1 7.05 us: on_device(): jnp.einsum('ktc,krc->ktr', picked, blocks, preferred_element_type=jnp.flo...]
    reduce_scatter x1 -> x0, waiting for transfers between devices: 10.9 us -> none  [on_device(): lax.psum_scatter(gradient_slab, 'mp', scatter_dimension=0, tiled=True)]
    unnamed x8 -> x13, local copies, waits for them, and re-layouts: 0.02 us -> 6.32 us
    gather x2 -> x0, local copies, waits for them, and re-layouts: 1.9 us -> none  [the longest x1 0.95 us: on_device(): resid_rows = jnp.take(residual, row_ids, axis=0)]
  transfers between devices with their start and end apart: 2 -> 0, of which waited for: 2 -> 0; matrix products, arithmetic and copies ran while one was open for 0% -> 0% of each run, Pallas kernels for 0% -> 0%
where the time goes in v1:
time: 45.7 us; the launch traced here: 45.3 us
  Pallas kernels  35.2 us (77%)
  local copies, waits for them, and re-layouts  6.32 us (14%)
  other arithmetic  3.07 us (7%)
  between operations  0.71 us (2%)
    pallas_call x1, Pallas kernels, on_device(): pl.pallas_call(functools.partial(kernel, n_mp, n_survey), out_shape=jax.S...  35.2 us
    unnamed x13, local copies, waits for them, and re-layouts  6.32 us
    reduce_max x2, other arithmetic, links(): return jnp.max(jnp.where(hit, at[None, :] + 1, 0), axis=1)  1.73 us
    concatenate x2, other arithmetic, links(): wanted = jnp.concatenate([ids, jnp.arange(count, dtype=jnp.int32)])  1.33 us

profile of v1, /device:TPU:0, one launch (start us, length us, event | category | flops | bytes accessed | tf_op | source)
XLA Modules:
  0.0 45.3 jit_solution(10255265417657101446)
XLA Ops:
  0.7 0.7 %pad_add_fusion.1 = s32[132]{0:T(256)S(1)} fusion(s32[4]{0:T(128)S(1)} %iota.25, s32[128]{0:T(128)} %bitcast.9), kind=kLoop, calls=%fused_computation.9 | loop fusion | flops 132 | bytes 1056 | tf_op jit(solution)/shard_map/concatenate | solution.py:205
  1.4 0.9 %select_reduce_fusion.1.col_links = s32[132]{0:T(256)S(1)} fusion(s32[128]{0:T(128)S(1)} %iota_add_fusion, s32[132]{0:T(256)} %constant.11.clone.1, s32[128]{0:T(128)} %bitcast.10, s32[132]{0:T(256)S(1)} %pad_add_fusion.1, pred[128]{0:T(512)(128)(4,1)S(1)} %iota_compare_fusion.2), kind=kLoop, calls=%fused_computation.4 | loop fusion | flops 101244 | bytes 2736 | tf_op jit(solution)/shard_map/reduce_max | solution.py:208
  2.2 0.7 %pad_add_fusion = s32[144]{0:T(256)S(1)} fusion(s32[16]{0:T(128)S(1)} %iota.22, s32[128]{0:T(128)} %bitcast.6), kind=kLoop, calls=%fused_computation.8 | loop fusion | flops 144 | bytes 1152 | tf_op jit(solution)/shard_map/concatenate | solution.py:205
  2.9 0.9 %select_reduce_fusion.row_links = s32[144]{0:T(256)S(1)} fusion(s32[128]{0:T(128)S(1)} %iota_add_fusion, s32[144]{0:T(256)} %constant.2.clone.1, s32[128]{0:T(128)} %bitcast.7, s32[144]{0:T(256)S(1)} %pad_add_fusion, pred[128]{0:T(512)(128)(4,1)S(1)} %iota_compare_fusion.2), kind=kLoop, calls=%fused_computation | loop fusion | flops 110448 | bytes 2880 | tf_op jit(solution)/shard_map/reduce_max | solution.py:208
  3.8 0.0 copy-start
  3.8 2.2 %copy-done = bf16[1,128,128,128]{3,2,1,0:T(8,128)(2,1)S(1)} copy-done((bf16[1,128,128,128]{3,2,1,0:T(8,128)(2,1)S(1)}, bf16[1,128,128,128]{3,2,1,0:T(8,128)(2,1)}, u32[]{:S(2)}) %copy-start) | copy-done | bytes 4194328
  6.0 0.0 copy-start.1
  6.0 0.8 %copy-done.1 = bf16[2,64,128]{2,1,0:T(8,128)(2,1)S(1)} copy-done((bf16[2,64,128]{2,1,0:T(8,128)(2,1)S(1)}, bf16[2,64,128]{2,1,0:T(8,128)(2,1)}, u32[]{:S(2)}) %copy-start.1) | copy-done | bytes 32792
  6.7 0.0 copy-start.2
  6.7 0.7 %copy-done.2 = bf16[1,64,128]{2,1,0:T(8,128)(2,1)S(1)} copy-done((bf16[1,64,128]{2,1,0:T(8,128)(2,1)S(1)}, bf16[1,64,128]{2,1,0:T(8,128)(2,1)}, u32[]{:S(2)}) %copy-start.2) | copy-done | bytes 16408
  7.4 0.0 copy-start.3
  7.4 0.7 %copy-done.3 = bf16[1,64,128]{2,1,0:T(8,128)(2,1)S(1)} copy-done((bf16[1,64,128]{2,1,0:T(8,128)(2,1)S(1)}, bf16[1,64,128]{2,1,0:T(8,128)(2,1)}, u32[]{:S(2)}) %copy-start.3) | copy-done | bytes 16408
  8.1 0.0 copy-start.4
  8.2 0.7 %copy-done.4 = s32[1,128]{1,0:T(1,128)S(1)} copy-done((s32[1,128]{1,0:T(1,128)S(1)}, s32[1,128]{1,0:T(1,128)}, u32[]{:S(2)}) %copy-start.4) | copy-done | bytes 536
  8.8 0.0 copy-start.5
  8.8 0.7 %copy-done.5 = s32[1,128]{1,0:T(1,128)S(1)} copy-done((s32[1,128]{1,0:T(1,128)S(1)}, s32[1,128]{1,0:T(1,128)}, u32[]{:S(2)}) %copy-start.5) | copy-done | bytes 536
  9.5 35.2 %shard_map.73 = f32[2,64,128]{2,1,0:T(8,128)S(1)} custom-call(s32[128]{0:T(128)S(1)} %bitcast.8, s32[128]{0:T(128)S(1)} %bitcast.11, s32[144]{0:T(256)S(1)} %select_reduce_fusion.row_links, s32[132]{0:T(256)S(1)} %select_reduce_fusion.1.col_links, bf16[2,64,128]{2,1,0:T(8,128)(2,1)S(1)} %copy-done.1, bf16[1,64,128]{2,1,0:T(8,128)(2,1)S(1)} %copy-done.2, ...), custom_call_target="tpu_custom_call" | custom-call | tf_op jit(solution)/shard_map/pallas_call | solution.py:226
  44.7 0.6 %copy.10 = f32[2,64,128]{2,1,0:T(8,128)} copy(f32[2,64,128]{2,1,0:T(8,128)S(1)} %shard_map.73) | data formatting | bytes 131072
  (4 shorter events, 0.0 us)
Async XLA Ops:
  3.8 2.2 %copy-start = (bf16[1,128,128,128]{3,2,1,0:T(8,128)(2,1)S(1)}, bf16[1,128,128,128]{3,2,1,0:T(8,128)(2,1)}, u32[]{:S(2)}) copy-start(bf16[1,128,128,128]{3,2,1,0:T(8,128)(2,1)} %param.10) | copy-start | bytes 12582916
  6.0 0.8 %copy-start.1 = (bf16[2,64,128]{2,1,0:T(8,128)(2,1)S(1)}, bf16[2,64,128]{2,1,0:T(8,128)(2,1)}, u32[]{:S(2)}) copy-start(bf16[2,64,128]{2,1,0:T(8,128)(2,1)} %model_ref.1) | copy-start | bytes 98308
  6.7 0.7 %copy-start.2 = (bf16[1,64,128]{2,1,0:T(8,128)(2,1)S(1)}, bf16[1,64,128]{2,1,0:T(8,128)(2,1)}, u32[]{:S(2)}) copy-start(bf16[1,64,128]{2,1,0:T(8,128)(2,1)} %seen_ref.1) | copy-start | bytes 49156
  7.4 0.7 %copy-start.3 = (bf16[1,64,128]{2,1,0:T(8,128)(2,1)S(1)}, bf16[1,64,128]{2,1,0:T(8,128)(2,1)}, u32[]{:S(2)}) copy-start(bf16[1,64,128]{2,1,0:T(8,128)(2,1)} %weight_ref.1) | copy-start | bytes 49156
  8.1 0.7 %copy-start.4 = (s32[1,128]{1,0:T(1,128)S(1)}, s32[1,128]{1,0:T(1,128)}, u32[]{:S(2)}) copy-start(s32[1,128]{1,0:T(1,128)} %param.11) | copy-start | bytes 1540
  8.8 0.7 %copy-start.5 = (s32[1,128]{1,0:T(1,128)S(1)}, s32[1,128]{1,0:T(1,128)}, u32[]{:S(2)}) copy-start(s32[1,128]{1,0:T(1,128)} %param.12) | copy-start | bytes 1540

commit v2 on v1

--- a/solution.py
+++ b/solution.py
@@ -21,16 +21,30 @@
     return SMOOTH * (2.0 * field - earlier - later_step)
 
 
+def link_tables(ids, count):
+    slots = ids.shape[1]
+    wide = jnp.broadcast_to(ids, (slots, slots))
+    tall = wide.T
+    j = lax.broadcasted_iota(jnp.int32, (slots, slots), 0)
+    q = lax.broadcasted_iota(jnp.int32, (slots, slots), 1)
+    at = jnp.where(j < count, j + 1, 0)
+    before = jnp.max(jnp.where((tall == wide) & (j < q), at, 0), axis=0, keepdims=True)
+    last = jnp.max(jnp.where(tall == q, at, 0), axis=0, keepdims=True)
+    return before, last
+
+
+ROW, ROW_BEFORE, ROW_LAST, COL, COL_BEFORE, COL_LAST = range(6)
+
+
 def kernel(
     n_mp,
     n_survey,
-    rows_ref,
-    cols_ref,
-    row_links,
-    col_links,
-    model_ref,
-    seen_ref,
-    weight_ref,
+    rows_hbm,
+    cols_hbm,
+    count_hbm,
+    model_hbm,
+    seen_hbm,
+    weight_hbm,
     sens_hbm,
     out_ref,
     blocks,
@@ -43,7 +57,15 @@
     resid,
     grad_send,
     grad_recv,
+    model_ref,
+    seen_ref,
+    weight_ref,
+    ids_ref,
+    count_ref,
+    tables,
+    table,
     load_sem,
+    small_sem,
     model_sem,
     sib_sem,
     chip_sem,
@@ -74,35 +96,61 @@
             device_id_type=MESH,
         )
 
+    smalls = [
+        pltpu.make_async_copy(src, dst, small_sem.at[i])
+        for i, (src, dst) in enumerate(
+            (
+                (count_hbm, count_ref),
+                (rows_hbm, ids_ref.at[0]),
+                (cols_hbm, ids_ref.at[1]),
+                (model_hbm, model_ref),
+                (seen_hbm, seen_ref),
+                (weight_hbm, weight_ref),
+            )
+        )
+    ]
     step = slots // PARTS
     loads = [
         pltpu.make_async_copy(
-            sens_hbm.at[pl.ds(i * step, step)], blocks.at[pl.ds(i * step, step)], load_sem.at[i]
+            sens_hbm.at[0, pl.ds(i * step, step)], blocks.at[pl.ds(i * step, step)], load_sem.at[i]
         )
         for i in range(PARTS)
     ]
-    for load in loads:
-        load.start()
 
     barrier = pltpu.get_barrier_semaphore()
     partners = [((m + j) % n_mp, s) for j in range(1, n_mp)] + [sibling]
     partners += [(m, chip_at(j) * 2 + core) for j in range(1, chips)]
     for partner in partners:
         pl.semaphore_signal(barrier, inc=1, device_id=partner, device_id_type=MESH)
+    for load in smalls + loads:
+        load.start()
+
+    for small in smalls[:3]:
+        small.wait()
+    count = count_ref[0, 0]
+    for base, which in ((ROW, 0), (COL, 1)):
+        ids = ids_ref[which]
+        before, last = link_tables(ids, count)
+        tables[pl.ds(base, 1)] = ids
+        tables[pl.ds(base + 1, 1)] = before
+        tables[pl.ds(base + 2, 1)] = last
+    to_scalars = pltpu.make_async_copy(tables, table, small_sem.at[6])
+    to_scalars.start()
     pl.semaphore_wait(barrier, len(partners))
 
     here = pl.ds(m * owned, owned)
     sends = [
-        copy(model_ref, slab.at[here], model_sem, j - 1, ((m + j) % n_mp, s))
+        copy(model_hbm, slab.at[here], model_sem, j - 1, ((m + j) % n_mp, s))
         for j in range(1, n_mp)
     ]
     for send in sends:
         send.start()
+    smalls[3].wait()
     slab[here] = model_ref[...]
     for i in range(owned):
         out_ref[i] = smoothing(model_ref[i].astype(jnp.float32))
     chain[0] = jnp.zeros(chain.shape[1:], jnp.float32)
-    for load in loads:
+    for load in loads + [to_scalars] + smalls[4:]:
         load.wait()
     for send in sends:
         send.wait()
@@ -111,7 +159,7 @@
         base = g * UNROLL
         terms = [
             lax.dot_general(
-                slab[cols_ref[base + u]],
+                slab[table[COL, base + u]],
                 blocks[base + u],
                 (((1,), (1,)), ((), ())),
                 preferred_element_type=jnp.float32,
@@ -119,7 +167,7 @@
             for u in range(UNROLL)
         ]
         for u in range(UNROLL):
-            chain[base + u + 1] = terms[u] + chain[row_links[base + u]]
+            chain[base + u + 1] = terms[u] + chain[table[ROW_BEFORE, base + u]]
         return carry
 
     lax.fori_loop(0, slots // UNROLL, forward, 0)
@@ -128,14 +176,14 @@
     swaps = {}
     for j in order:
         for i in range(per):
-            sib_send[j, i] = chain[row_links[slots + (chip_at(j) * 2 + 1 - core) * per + i]]
+            sib_send[j, i] = chain[table[ROW_LAST, (chip_at(j) * 2 + 1 - core) * per + i]]
         swaps[j] = copy(sib_send.at[j], sib_recv.at[j], sib_sem, j, sibling)
         swaps[j].start()
     scatters = {}
     for j in order:
         swaps[j].wait_recv()
         for i in range(per):
-            mine = chain[row_links[slots + (chip_at(j) * 2 + core) * per + i]]
+            mine = chain[table[ROW_LAST, (chip_at(j) * 2 + core) * per + i]]
             chip_send[j, i] = mine + sib_recv[j, i]
         if j:
             scatters[j] = copy(
@@ -170,12 +218,12 @@
         base = g * UNROLL
         terms = [
             jnp.dot(
-                resid[rows_ref[base + u]], blocks[base + u], preferred_element_type=jnp.float32
+                resid[table[ROW, base + u]], blocks[base + u], preferred_element_type=jnp.float32
             )
             for u in range(UNROLL)
         ]
         for u in range(UNROLL):
-            chain[base + u + 1] = terms[u] + chain[col_links[base + u]]
+            chain[base + u + 1] = terms[u] + chain[table[COL_BEFORE, base + u]]
         return carry
 
     lax.fori_loop(0, slots // UNROLL, backward, 0)
@@ -184,11 +232,11 @@
     for j in range(1, n_mp):
         owner = (m + j) % n_mp
         for i in range(owned):
-            grad_send[j, i] = chain[col_links[slots + owner * owned + i]]
+            grad_send[j, i] = chain[table[COL_LAST, owner * owned + i]]
         returns[j] = copy(grad_send.at[j], grad_recv.at[j], grad_sem, j, (owner, s))
         returns[j].start()
     for i in range(owned):
-        out_ref[i] += chain[col_links[slots + m * owned + i]]
+        out_ref[i] += chain[table[COL_LAST, m * owned + i]]
     for j in range(1, n_mp):
         returns[j].wait_recv()
         out_ref[...] += grad_recv[j]
@@ -199,35 +247,20 @@
             sent.wait_send()
 
 
-def links(ids, in_use, count):
-    slots = ids.shape[0]
-    at = jnp.arange(slots, dtype=jnp.int32)
-    wanted = jnp.concatenate([ids, jnp.arange(count, dtype=jnp.int32)])
-    limit = jnp.concatenate([at, jnp.full((count,), slots, jnp.int32)])
-    hit = (wanted[:, None] == ids[None, :]) & (at[None, :] < limit[:, None]) & in_use[None, :]
-    return jnp.max(jnp.where(hit, at[None, :] + 1, 0), axis=1)
-
-
 def on_device(
     n_mp, n_survey, model, observed, weights, sensitivity, block_rows, block_cols, block_count
 ):
-    row_ids, col_ids = block_rows[0], block_cols[0]
-    slots = row_ids.shape[0]
+    slots = block_rows.shape[1]
     owned, steps, cells = model.shape
     per = observed.shape[0]
     chips = n_survey // 2
-    in_use = jnp.arange(slots, dtype=jnp.int32) < block_count[0, 0]
-    row_links = links(row_ids, in_use, per * n_survey)
-    col_links = links(col_ids, in_use, owned * n_mp)
-    smem = pl.BlockSpec(memory_space=pltpu.SMEM)
-    vmem = pl.BlockSpec(memory_space=pltpu.VMEM)
     pair = lambda n: pltpu.SemaphoreType.DMA((2, n))
-    f32, bf16 = jnp.float32, jnp.bfloat16
+    f32, bf16, i32 = jnp.float32, jnp.bfloat16, jnp.int32
     return pl.pallas_call(
         functools.partial(kernel, n_mp, n_survey),
         out_shape=jax.ShapeDtypeStruct(model.shape, f32),
-        in_specs=[smem] * 4 + [vmem] * 3 + [pl.BlockSpec(memory_space=pl.ANY)],
-        out_specs=vmem,
+        in_specs=[pl.BlockSpec(memory_space=pl.ANY)] * 7,
+        out_specs=pl.BlockSpec(memory_space=pltpu.VMEM),
         scratch_shapes=[
             pltpu.VMEM(sensitivity.shape[1:], bf16),
             pltpu.VMEM((owned * n_mp, steps, cells), bf16),
@@ -239,7 +272,15 @@
             pltpu.VMEM((per * n_survey, steps, cells), bf16),
             pltpu.VMEM((n_mp, owned, steps, cells), f32),
             pltpu.VMEM((n_mp, owned, steps, cells), f32),
+            pltpu.VMEM(model.shape, bf16),
+            pltpu.VMEM(observed.shape, bf16),
+            pltpu.VMEM(weights.shape, bf16),
+            pltpu.VMEM((2, 1, slots), i32),
+            pltpu.SMEM((1, 1), i32),
+            pltpu.VMEM((8, slots), i32),
+            pltpu.SMEM((8, slots), i32),
             pltpu.SemaphoreType.DMA((PARTS,)),
+            pltpu.SemaphoreType.DMA((7,)),
             pair(n_mp),
             pair(chips),
             pair(chips),
@@ -249,9 +290,9 @@
             pair(n_mp),
         ],
         compiler_params=pltpu.CompilerParams(
-            collective_id=0, has_side_effects=True, vmem_limit_bytes=40 << 20
+            collective_id=0, has_side_effects=True, vmem_limit_bytes=60 << 20
         ),
-    )(row_ids, col_ids, row_links, col_links, model, observed, weights, sensitivity[0])
+    )(block_rows, block_cols, block_count, model, observed, weights, sensitivity)
 
 
 def solution(mesh):

time: 45.7 us -> 37 us (0.81)
  local copies, waits for them, and re-layouts: 6.32 us -> 1.47 us
  other arithmetic: 3.07 us -> 0 us
  Pallas kernels: 35.2 us -> 34.7 us
    unnamed x13 -> x1, local copies, waits for them, and re-layouts: 6.32 us -> 1.47 us
    reduce_max x2 -> x0, other arithmetic: 1.73 us -> none  [links(): return jnp.max(jnp.where(hit, at[None, :] + 1, 0), axis=1)]
    concatenate x2 -> x0, other arithmetic: 1.33 us -> none  [links(): wanted = jnp.concatenate([ids, jnp.arange(count, dtype=jnp.int32)])]
    pallas_call x1, Pallas kernels: 35.2 us -> 34.7 us  [on_device(): pl.pallas_call(functools.partial(kernel, n_mp, n_survey), out_shape=jax.S...]
where the time goes in v2:
time: 37 us; the launch traced here: 36.8 us
  Pallas kernels  34.7 us (94%)
  local copies, waits for them, and re-layouts  1.47 us (4%)
  between operations  0.66 us (2%)
    pallas_call x1, Pallas kernels, on_device(): pl.pallas_call(functools.partial(kernel, n_mp, n_survey), out_shape=jax.S...  34.7 us
    unnamed x1, local copies, waits for them, and re-layouts  1.47 us

profile of v2, /device:TPU:0, one launch (start us, length us, event | category | flops | bytes accessed | tf_op | source)
XLA Modules:
  0.0 36.8 jit_solution(11702936348634495130)
XLA Ops:
  0.7 34.7 %shard_map.73 = f32[2,64,128]{2,1,0:T(8,128)} custom-call(s32[1,128]{1,0:T(1,128)} %rows_hbm.1, s32[1,128]{1,0:T(1,128)} %cols_hbm.1, s32[1,1]{1,0:T(1,128)S(6)} %copy.9.count_hbm, bf16[2,64,128]{2,1,0:T(8,128)(2,1)} %model_hbm.1, bf16[1,64,128]{2,1,0:T(8,128)(2,1)} %seen_hbm.1, bf16[1,64,128]{2,1,0:T(8,128)(2,1)} %weight_hbm.1, ...), custom_call_target="tpu_custom_call" | custom-call | tf_op jit(solution)/shard_map/pallas_call | solution.py:259
  35.3 1.5 %copy.10 = f32[2,64,128]{2,1,0:T(8,128)} copy(f32[2,64,128]{2,1,0:T(8,128)} %shard_map.73) | data formatting | bytes 131072

commit v3 on v2

--- a/solution.py
+++ b/solution.py
@@ -10,7 +10,8 @@
 SMOOTH = 0.5
 MESH = pl.DeviceIdType.MESH
 PARTS = 8
-UNROLL = 8
+UNROLL = 64
+SWAPS = 2
 
 
 def smoothing(field):
@@ -69,7 +70,6 @@
     model_sem,
     sib_sem,
     chip_sem,
-    own_sem,
     gather_sem,
     relay_sem,
     grad_sem,
@@ -109,10 +109,10 @@
             )
         )
     ]
-    step = slots // PARTS
+    part = slots // PARTS
     loads = [
         pltpu.make_async_copy(
-            sens_hbm.at[0, pl.ds(i * step, step)], blocks.at[pl.ds(i * step, step)], load_sem.at[i]
+            sens_hbm.at[0, pl.ds(i * part, part)], blocks.at[pl.ds(i * part, part)], load_sem.at[i]
         )
         for i in range(PARTS)
     ]
@@ -130,6 +130,9 @@
     count = count_ref[0, 0]
     for base, which in ((ROW, 0), (COL, 1)):
         ids = ids_ref[which]
+        if base == ROW:
+            owner = ids // per
+            ids = (owner % 2 * chips + owner // 2) * per + ids % per
         before, last = link_tables(ids, count)
         tables[pl.ds(base, 1)] = ids
         tables[pl.ds(base + 1, 1)] = before
@@ -155,80 +158,89 @@
     for send in sends:
         send.wait()
 
-    def forward(g, carry):
-        base = g * UNROLL
-        terms = [
-            lax.dot_general(
-                slab[table[COL, base + u]],
-                blocks[base + u],
-                (((1,), (1,)), ((), ())),
-                preferred_element_type=jnp.float32,
-            )
-            for u in range(UNROLL)
-        ]
-        for u in range(UNROLL):
-            chain[base + u + 1] = terms[u] + chain[table[ROW_BEFORE, base + u]]
-        return carry
-
-    lax.fori_loop(0, slots // UNROLL, forward, 0)
+    def forward():
+        def body(g, carry):
+            base = g * UNROLL
+            terms = [
+                lax.dot_general(
+                    slab[table[COL, base + u]],
+                    blocks[base + u],
+                    (((1,), (1,)), ((), ())),
+                    preferred_element_type=jnp.float32,
+                )
+                for u in range(UNROLL)
+            ]
+            for u in range(UNROLL):
+                before = chain[table[ROW_BEFORE, base + u]]
+                chain[base + u + 1] = terms[u] + before
+            return carry
+
+        lax.fori_loop(0, slots // UNROLL, body, 0)
+
+    def backward():
+        def body(g, carry):
+            base = g * UNROLL
+            terms = [
+                jnp.dot(
+                    resid[table[ROW, base + u]],
+                    blocks[base + u],
+                    preferred_element_type=jnp.float32,
+                )
+                for u in range(UNROLL)
+            ]
+            for u in range(UNROLL):
+                before = chain[table[COL_BEFORE, base + u]]
+                chain[base + u + 1] = terms[u] + before
+            return carry
+
+        lax.fori_loop(0, slots // UNROLL, body, 0)
+
+    forward()
 
     order = list(range(1, chips)) + [0]
-    swaps = {}
-    for j in order:
+    group = chips // SWAPS
+    swaps, scatters, gathers, returns = {}, {}, {}, {}
+    for p, j in enumerate(order):
         for i in range(per):
-            sib_send[j, i] = chain[table[ROW_LAST, (chip_at(j) * 2 + 1 - core) * per + i]]
-        swaps[j] = copy(sib_send.at[j], sib_recv.at[j], sib_sem, j, sibling)
-        swaps[j].start()
-    scatters = {}
-    for j in order:
-        swaps[j].wait_recv()
+            row = ((1 - core) * chips + chip_at(j)) * per + i
+            sib_send[p, i] = chain[table[ROW_LAST, row]]
+        if (p + 1) % group == 0:
+            some = pl.ds(p + 1 - group, group)
+            swaps[p] = copy(sib_send.at[some], sib_recv.at[some], sib_sem, p, sibling)
+            swaps[p].start()
+    for p, j in enumerate(order):
+        if p % group == 0:
+            swaps[p + group - 1].wait_recv()
         for i in range(per):
-            mine = chain[table[ROW_LAST, (chip_at(j) * 2 + core) * per + i]]
-            chip_send[j, i] = mine + sib_recv[j, i]
+            row = (core * chips + chip_at(j)) * per + i
+            chip_send[j, i] = chain[table[ROW_LAST, row]] + sib_recv[p, i]
         if j:
             scatters[j] = copy(
                 chip_send.at[j], chip_recv.at[j], chip_sem, j, (m, chip_at(j) * 2 + core)
             )
             scatters[j].start()
+
     total = chip_send[0]
     for j in range(1, chips):
         scatters[j].wait_recv()
         total += chip_recv[j]
-
     value = weight_ref[...].astype(jnp.float32) * (total - seen_ref[...].astype(jnp.float32))
-    mine = resid.at[pl.ds(s * per, per)]
-    resid[pl.ds(s * per, per)] = value.astype(jnp.bfloat16)
-    gathers = {}
+    here = pl.ds((core * chips + chip) * per, per)
+    resid[here] = value.astype(jnp.bfloat16)
     for j in range(1, chips):
-        gathers[j] = copy(mine, mine, gather_sem, j, (m, chip_at(j) * 2 + core))
+        gathers[j] = copy(
+            resid.at[here], resid.at[here], gather_sem, j, (m, chip_at(j) * 2 + core)
+        )
         gathers[j].start()
-    own = copy(mine, mine, own_sem, 0, sibling)
-    own.start()
-    relays = {}
     for j in range(1, chips):
         gathers[j].wait_recv()
-        source = resid.at[pl.ds((chip_at(chips - j) * 2 + core) * per, per)]
-        relays[j] = copy(source, source, relay_sem, j, sibling)
-        relays[j].start()
-    own.wait_recv()
-    for j in range(1, chips):
-        relays[j].wait_recv()
-
-    def backward(g, carry):
-        base = g * UNROLL
-        terms = [
-            jnp.dot(
-                resid[table[ROW, base + u]], blocks[base + u], preferred_element_type=jnp.float32
-            )
-            for u in range(UNROLL)
-        ]
-        for u in range(UNROLL):
-            chain[base + u + 1] = terms[u] + chain[table[COL_BEFORE, base + u]]
-        return carry
-
-    lax.fori_loop(0, slots // UNROLL, backward, 0)
-
-    returns = {}
+    same = resid.at[pl.ds(core * chips * per, chips * per)]
+    relay = copy(same, same, relay_sem, 0, sibling)
+    relay.start()
+    relay.wait_recv()
+
+    backward()
+
     for j in range(1, n_mp):
         owner = (m + j) % n_mp
         for i in range(owned):
@@ -241,10 +253,10 @@
         returns[j].wait_recv()
         out_ref[...] += grad_recv[j]
 
-    own.wait_send()
-    for group in (swaps, scatters, gathers, relays, returns):
-        for sent in group.values():
-            sent.wait_send()
+    relay.wait_send()
+    for sent in (swaps, scatters, gathers, returns):
+        for one in sent.values():
+            one.wait_send()
 
 
 def on_device(
@@ -284,7 +296,6 @@
             pair(n_mp),
             pair(chips),
             pair(chips),
-            pair(1),
             pair(chips),
             pair(chips),
             pair(n_mp),

time: 37 us -> 33.7 us (0.911)
  Pallas kernels: 34.7 us -> 31.4 us
    pallas_call x1, Pallas kernels: 34.7 us -> 31.4 us  [on_device(): pl.pallas_call(functools.partial(kernel, n_mp, n_survey), out_shape=jax.S...]
where the time goes in v3:
time: 33.7 us; the launch traced here: 33.6 us
  Pallas kernels  31.4 us (93%)
  local copies, waits for them, and re-layouts  1.47 us (4%)
  between operations  0.66 us (2%)
    pallas_call x1, Pallas kernels, on_device(): pl.pallas_call(functools.partial(kernel, n_mp, n_survey), out_shape=jax.S...  31.4 us
    unnamed x1, local copies, waits for them, and re-layouts  1.47 us

profile of v3, /device:TPU:0, one launch (start us, length us, event | category | flops | bytes accessed | tf_op | source)
XLA Modules:
  0.0 33.6 jit_solution(654928226748388721)
XLA Ops:
  0.7 31.4 %shard_map.73 = f32[2,64,128]{2,1,0:T(8,128)} custom-call(s32[1,128]{1,0:T(1,128)} %rows_hbm.1, s32[1,128]{1,0:T(1,128)} %cols_hbm.1, s32[1,1]{1,0:T(1,128)S(6)} %copy.9.count_hbm, bf16[2,64,128]{2,1,0:T(8,128)(2,1)} %model_hbm.1, bf16[1,64,128]{2,1,0:T(8,128)(2,1)} %seen_hbm.1, bf16[1,64,128]{2,1,0:T(8,128)(2,1)} %weight_hbm.1, ...), custom_call_target="tpu_custom_call" | custom-call | tf_op jit(solution)/shard_map/pallas_call | solution.py:271
  32.1 1.5 %copy.10 = f32[2,64,128]{2,1,0:T(8,128)} copy(f32[2,64,128]{2,1,0:T(8,128)} %shard_map.73) | data formatting | bytes 131072

commit v4 on v3

--- a/solution.py
+++ b/solution.py
@@ -12,6 +12,7 @@
 PARTS = 8
 UNROLL = 64
 SWAPS = 2
+LIMIT = 32
 
 
 def smoothing(field):
@@ -37,77 +38,37 @@
 ROW, ROW_BEFORE, ROW_LAST, COL, COL_BEFORE, COL_LAST = range(6)
 
 
-def kernel(
-    n_mp,
-    n_survey,
-    rows_hbm,
-    cols_hbm,
-    count_hbm,
-    model_hbm,
-    seen_hbm,
-    weight_hbm,
-    sens_hbm,
-    out_ref,
-    blocks,
-    slab,
-    chain,
-    sib_send,
-    sib_recv,
-    chip_send,
-    chip_recv,
-    resid,
-    grad_send,
-    grad_recv,
-    model_ref,
-    seen_ref,
-    weight_ref,
-    ids_ref,
-    count_ref,
-    tables,
-    table,
-    load_sem,
-    small_sem,
-    model_sem,
-    sib_sem,
-    chip_sem,
-    gather_sem,
-    relay_sem,
-    grad_sem,
+def copy(src, dst, sems, j, device):
+    return pltpu.make_async_remote_copy(
+        src_ref=src,
+        dst_ref=dst,
+        send_sem=sems.at[0, j],
+        recv_sem=sems.at[1, j],
+        device_id=device,
+        device_id_type=MESH,
+    )
+
+
+def collect(
+    n_mp, n_survey, per, rows_hbm, cols_hbm, count_hbm, model_hbm, sens_hbm,
+    table, slab, blocks, ids_ref, count_ref, tables, load_sem, small_sem, model_sem,
 ):
     m = lax.axis_index("mp")
     s = lax.axis_index("survey")
     chips = n_survey // 2
-    chip, core = s // 2, s % 2
-    sibling = (m, chip * 2 + 1 - core)
     slots = blocks.shape[0]
-    owned = model_ref.shape[0]
-    per = seen_ref.shape[0]
-
-    def chip_at(j):
-        return (chip + j) % chips
-
-    def copy(src, dst, sems, j, device):
-        return pltpu.make_async_remote_copy(
-            src_ref=src,
-            dst_ref=dst,
-            send_sem=sems.at[0, j],
-            recv_sem=sems.at[1, j],
-            device_id=device,
-            device_id_type=MESH,
+    owned = model_hbm.shape[0]
+    here = pl.ds(m * owned, owned)
+    barrier = pltpu.get_barrier_semaphore()
+    for j in range(1, n_mp):
+        pl.semaphore_signal(
+            barrier, inc=1, device_id=((m + j) % n_mp, s), device_id_type=MESH
         )
-
     smalls = [
-        pltpu.make_async_copy(src, dst, small_sem.at[i])
-        for i, (src, dst) in enumerate(
-            (
-                (count_hbm, count_ref),
-                (rows_hbm, ids_ref.at[0]),
-                (cols_hbm, ids_ref.at[1]),
-                (model_hbm, model_ref),
-                (seen_hbm, seen_ref),
-                (weight_hbm, weight_ref),
-            )
-        )
+        pltpu.make_async_copy(count_hbm, count_ref, small_sem.at[0]),
+        pltpu.make_async_copy(rows_hbm, ids_ref.at[0], small_sem.at[1]),
+        pltpu.make_async_copy(cols_hbm, ids_ref.at[1], small_sem.at[2]),
+        pltpu.make_async_copy(model_hbm, slab.at[here], small_sem.at[3]),
     ]
     part = slots // PARTS
     loads = [
@@ -116,15 +77,8 @@
         )
         for i in range(PARTS)
     ]
-
-    barrier = pltpu.get_barrier_semaphore()
-    partners = [((m + j) % n_mp, s) for j in range(1, n_mp)] + [sibling]
-    partners += [(m, chip_at(j) * 2 + core) for j in range(1, chips)]
-    for partner in partners:
-        pl.semaphore_signal(barrier, inc=1, device_id=partner, device_id_type=MESH)
     for load in smalls + loads:
         load.start()
-
     for small in smalls[:3]:
         small.wait()
     count = count_ref[0, 0]
@@ -137,26 +91,47 @@
         tables[pl.ds(base, 1)] = ids
         tables[pl.ds(base + 1, 1)] = before
         tables[pl.ds(base + 2, 1)] = last
-    to_scalars = pltpu.make_async_copy(tables, table, small_sem.at[6])
+    to_scalars = pltpu.make_async_copy(tables, table, small_sem.at[4])
     to_scalars.start()
-    pl.semaphore_wait(barrier, len(partners))
-
-    here = pl.ds(m * owned, owned)
+    if n_mp > 1:
+        pl.semaphore_wait(barrier, n_mp - 1)
     sends = [
         copy(model_hbm, slab.at[here], model_sem, j - 1, ((m + j) % n_mp, s))
         for j in range(1, n_mp)
     ]
     for send in sends:
         send.start()
-    smalls[3].wait()
-    slab[here] = model_ref[...]
+    for load in loads + [to_scalars, smalls[3]]:
+        load.wait()
+    for send in sends:
+        send.wait()
+
+
+def kernel(
+    n_mp, n_survey, table, slab, blocks, model_ref, seen_ref, weight_ref, out_ref,
+    chain, sib_send, sib_recv, chip_send, chip_recv, resid, grad_send, grad_recv,
+    sib_sem, chip_sem, gather_sem, relay_sem, grad_sem,
+):
+    m = lax.axis_index("mp")
+    s = lax.axis_index("survey")
+    chips = n_survey // 2
+    chip, core = s // 2, s % 2
+    sibling = (m, chip * 2 + 1 - core)
+    slots = blocks.shape[0]
+    owned = model_ref.shape[0]
+    per = seen_ref.shape[0]
+
+    def chip_at(j):
+        return (chip + j) % chips
+
+    barrier = pltpu.get_barrier_semaphore()
+    partners = [((m + j) % n_mp, s) for j in range(1, n_mp)] + [sibling]
+    partners += [(m, chip_at(j) * 2 + core) for j in range(1, chips)]
+    for partner in partners:
+        pl.semaphore_signal(barrier, inc=1, device_id=partner, device_id_type=MESH)
     for i in range(owned):
         out_ref[i] = smoothing(model_ref[i].astype(jnp.float32))
     chain[0] = jnp.zeros(chain.shape[1:], jnp.float32)
-    for load in loads + [to_scalars] + smalls[4:]:
-        load.wait()
-    for send in sends:
-        send.wait()
 
     def forward():
         def body(g, carry):
@@ -196,6 +171,7 @@
         lax.fori_loop(0, slots // UNROLL, body, 0)
 
     forward()
+    pl.semaphore_wait(barrier, len(partners))
 
     order = list(range(1, chips)) + [0]
     group = chips // SWAPS
@@ -268,32 +244,46 @@
     chips = n_survey // 2
     pair = lambda n: pltpu.SemaphoreType.DMA((2, n))
     f32, bf16, i32 = jnp.float32, jnp.bfloat16, jnp.int32
+    hbm = pl.BlockSpec(memory_space=pl.ANY)
+    smem = pl.BlockSpec(memory_space=pltpu.SMEM)
+    vmem = pl.BlockSpec(memory_space=pltpu.VMEM)
+    keep = lambda x: pltpu.with_memory_space_constraint(x, pltpu.HBM)
+    share = pltpu.VMEM((chips, per, steps, cells), f32)
+    table, slab, blocks = pl.pallas_call(
+        functools.partial(collect, n_mp, n_survey, per),
+        out_shape=[
+            jax.ShapeDtypeStruct((8, slots), i32),
+            jax.ShapeDtypeStruct((owned * n_mp, steps, cells), bf16),
+            jax.ShapeDtypeStruct(sensitivity.shape[1:], bf16),
+        ],
+        in_specs=[hbm] * 5,
+        out_specs=[smem, vmem, vmem],
+        scratch_shapes=[
+            pltpu.VMEM((2, 1, slots), i32),
+            pltpu.SMEM((1, 1), i32),
+            pltpu.VMEM((8, slots), i32),
+            pltpu.SemaphoreType.DMA((PARTS,)),
+            pltpu.SemaphoreType.DMA((5,)),
+            pair(n_mp),
+        ],
+        compiler_params=pltpu.CompilerParams(
+            collective_id=0, has_side_effects=True, vmem_limit_bytes=LIMIT << 20
+        ),
+    )(keep(block_rows), keep(block_cols), block_count, keep(model), keep(sensitivity))
     return pl.pallas_call(
         functools.partial(kernel, n_mp, n_survey),
         out_shape=jax.ShapeDtypeStruct(model.shape, f32),
-        in_specs=[pl.BlockSpec(memory_space=pl.ANY)] * 7,
-        out_specs=pl.BlockSpec(memory_space=pltpu.VMEM),
+        in_specs=[smem] + [vmem] * 5,
+        out_specs=vmem,
         scratch_shapes=[
-            pltpu.VMEM(sensitivity.shape[1:], bf16),
-            pltpu.VMEM((owned * n_mp, steps, cells), bf16),
             pltpu.VMEM((slots + 1, steps, cells), f32),
-            pltpu.VMEM((chips, per, steps, cells), f32),
-            pltpu.VMEM((chips, per, steps, cells), f32),
-            pltpu.VMEM((chips, per, steps, cells), f32),
-            pltpu.VMEM((chips, per, steps, cells), f32),
+            share,
+            share,
+            share,
+            share,
             pltpu.VMEM((per * n_survey, steps, cells), bf16),
             pltpu.VMEM((n_mp, owned, steps, cells), f32),
             pltpu.VMEM((n_mp, owned, steps, cells), f32),
-            pltpu.VMEM(model.shape, bf16),
-            pltpu.VMEM(observed.shape, bf16),
-            pltpu.VMEM(weights.shape, bf16),
-            pltpu.VMEM((2, 1, slots), i32),
-            pltpu.SMEM((1, 1), i32),
-            pltpu.VMEM((8, slots), i32),
-            pltpu.SMEM((8, slots), i32),
-            pltpu.SemaphoreType.DMA((PARTS,)),
-            pltpu.SemaphoreType.DMA((7,)),
-            pair(n_mp),
             pair(chips),
             pair(chips),
             pair(chips),
@@ -301,9 +291,9 @@
             pair(n_mp),
         ],
         compiler_params=pltpu.CompilerParams(
-            collective_id=0, has_side_effects=True, vmem_limit_bytes=60 << 20
+            collective_id=1, has_side_effects=True, vmem_limit_bytes=LIMIT << 20
         ),
-    )(block_rows, block_cols, block_count, model, observed, weights, sensitivity)
+    )(table, slab, blocks, model, observed, weights)
 
 
 def solution(mesh):

time: 33.7 us -> 32.6 us (0.967)
  local copies, waits for them, and re-layouts: 1.47 us -> 0.64 us
    pallas_call x1, Pallas kernels: 31.4 us -> 23.4 us  [on_device(): pl.pallas_call(functools.partial(kernel, n_mp, n_survey), out_shape=jax.S...]
    pallas_call x0 -> x1, Pallas kernels: none -> 7.64 us  [on_device(): pl.pallas_call(functools.partial(collect, n_mp, n_survey, per), out_shape...]
    unnamed x1 -> x7, local copies, waits for them, and re-layouts: 1.47 us -> 0.64 us
where the time goes in v4:
time: 32.6 us; the launch traced here: 32.4 us
  Pallas kernels  31.1 us (95%)
  between operations  0.7 us (2%)
  local copies, waits for them, and re-layouts  0.64 us (2%)
    pallas_call x1, Pallas kernels, on_device(): pl.pallas_call(functools.partial(kernel, n_mp, n_survey), out_shape=jax.S...  23.4 us
    pallas_call x1, Pallas kernels, on_device(): pl.pallas_call(functools.partial(collect, n_mp, n_survey, per), out_shape...  7.64 us

profile of v4, /device:TPU:0, one launch (start us, length us, event | category | flops | bytes accessed | tf_op | source)
XLA Modules:
  0.0 32.4 jit_solution(8557644942229807470)
XLA Ops:
  0.0 0.0 copy-start
  0.0 0.0 copy-start.2
  0.0 0.0 copy-start.1
  0.7 7.6 %shard_map.73 = (s32[8,128]{1,0:T(8,128)S(1)}, bf16[4,64,128]{2,1,0:T(8,128)(2,1)S(1)}, bf16[128,128,128]{2,1,0:T(8,128)(2,1)S(1)}) custom-call(s32[1,128]{1,0:T(1,128)} %rows_hbm.1, s32[1,128]{1,0:T(1,128)} %cols_hbm.1, s32[1,1]{1,0:T(1,128)S(6)} %copy.9.count_hbm, bf16[2,64,128]{2,1,0:T(8,128)(2,1)} %model_ref.1, bf16[1,128,128,128]{3,2,1,0:T(8,128)(2,1)} %sens_hbm.1), custom_call_target="tpu_custom_call" | custom-call | tf_op jit(solution)/shard_map/pallas_call | solution.py:252
  8.3 0.0 copy-done
  8.3 0.0 copy-done.2
  8.3 0.0 copy-done.1
  8.3 23.4 %shard_map.74 = f32[2,64,128]{2,1,0:T(8,128)S(1)} custom-call(s32[8,128]{1,0:T(8,128)S(1)} %get-tuple-element.8.table, bf16[4,64,128]{2,1,0:T(8,128)(2,1)S(1)} %get-tuple-element.9.slab, bf16[128,128,128]{2,1,0:T(8,128)(2,1)S(1)} %get-tuple-element.10.blocks, bf16[2,64,128]{2,1,0:T(8,128)(2,1)S(1)} %copy-done, bf16[1,64,128]{2,1,0:T(8,128)(2,1)S(1)} %copy-done.1, ...), custom_call_target="tpu_custom_call" | custom-call | tf_op jit(solution)/shard_map/pallas_call | solution.py:273
  31.8 0.6 %copy.10 = f32[2,64,128]{2,1,0:T(8,128)} copy(f32[2,64,128]{2,1,0:T(8,128)S(1)} %shard_map.74) | data formatting | bytes 131072
Async XLA Ops:
  0.0 8.3 %copy-start = (bf16[2,64,128]{2,1,0:T(8,128)(2,1)S(1)}, bf16[2,64,128]{2,1,0:T(8,128)(2,1)}, u32[]{:S(2)}) copy-start(bf16[2,64,128]{2,1,0:T(8,128)(2,1)} %model_ref.1) | copy-start | bytes 98308
  0.0 8.3 %copy-start.2 = (bf16[1,64,128]{2,1,0:T(8,128)(2,1)S(1)}, bf16[1,64,128]{2,1,0:T(8,128)(2,1)}, u32[]{:S(2)}) copy-start(bf16[1,64,128]{2,1,0:T(8,128)(2,1)} %weight_ref.1) | copy-start | bytes 49156
  0.0 8.3 %copy-start.1 = (bf16[1,64,128]{2,1,0:T(8,128)(2,1)S(1)}, bf16[1,64,128]{2,1,0:T(8,128)(2,1)}, u32[]{:S(2)}) copy-start(bf16[1,64,128]{2,1,0:T(8,128)(2,1)} %seen_ref.1) | copy-start | bytes 49156
